TPU v7x, 256 devices: a whole 4x4x8 slice. The times are simulated.
256 devices in a mesh: seq: 32 (over y_lo, z, core), tp: 4 (over x), dp: 2 (over y_hi).
Axes of the slice: x: 4, y: 4 (y_hi: 2, y_lo: 2; y = y_hi * 2 + y_lo), z: 8, core: 2. Of those that a mesh axis runs over, the one named last changes fastest.
Arguments:
- query_gate: bfloat16 [2, 8192, 4096], P('dp', 'seq', 'tp'), may hold values from -6 to 6
- key_gate: bfloat16 [2, 8192, 4096], P('dp', 'seq', 'tp'), may hold values from -6 to 6
- value_input: bfloat16 [2, 8192, 4096], P('dp', 'seq', 'tp'), may hold values from -6 to 6
- filter_taps: bfloat16 [4096, 128], P('tp'), may hold values from -0.5 to 0.5
- skip_gain: float32 [4096], P('tp'), may hold values from -1 to 1
- out_weight: bfloat16 [4096, 4096], P('tp', 'dp'), may hold values from -0.09375 to 0.09375
- cotangent: bfloat16 [2, 8192, 4096], P('dp', 'seq', 'tp'), may hold values from -6 to 6
Outputs:
- grad_query: bfloat16 [2, 8192, 4096], P('dp', 'seq', 'tp')
- grad_key: bfloat16 [2, 8192, 4096], P('dp', 'seq', 'tp')
- grad_value: bfloat16 [2, 8192, 4096], P('dp', 'seq', 'tp')
- grad_filter: float32 [4096, 128], P('tp')
- grad_skip: float32 [4096], P('tp')
- grad_weight: float32 [4096, 4096], P(('seq', 'dp'), 'tp')
All inputs are finite; a program needn't handle non-finite values.
Results may differ from a plain program's by a relative error of at most 0.0095.
Values may be sent and summed in bfloat16 or wider, within the bound.
A program may use at most 192 MiB of HBM per device.

v0:
```python
import math
import jax
import jax.numpy as jnp
from jax import lax
from jax.sharding import PartitionSpec as P

block_rows = 16


def shifted(block, axis, distance):
    devices = range(lax.axis_size(axis))
    route = [(i - distance, i) for i in devices if i - distance in devices]
    return lax.ppermute(block, axis, route)


def taps_matrix(vector, row_count, col_count):
    channels, width_all = vector.shape
    tiled = jnp.tile(vector, (1, row_count + 1))
    skewed = tiled[:, : row_count * (width_all - 1)].reshape(channels, row_count, width_all - 1)
    return skewed[:, :, row_count - 1 : row_count - 1 + col_count]


def forward_table(filter_taps):
    channels, tap_count = filter_taps.shape
    padding = jnp.zeros((channels, block_rows), filter_taps.dtype)
    vector = jnp.concatenate([padding, filter_taps[:, ::-1], padding], axis=1)
    return taps_matrix(vector, block_rows, tap_count + block_rows)


def backward_table(filter_taps):
    channels, tap_count = filter_taps.shape
    before = jnp.zeros((channels, block_rows - 1), filter_taps.dtype)
    after = jnp.zeros((channels, block_rows + 1), filter_taps.dtype)
    vector = jnp.concatenate([before, filter_taps, after], axis=1)
    return taps_matrix(vector, block_rows, tap_count + block_rows)


def windows(extended, length, tap_count):
    pieces = []
    for shift_index in range(tap_count // block_rows + 1):
        lower = shift_index * block_rows
        pieces.append(
            extended[lower : lower + length].reshape(
                length // block_rows, block_rows, extended.shape[1]
            )
        )
    return jnp.concatenate(pieces, axis=1)


def lag_sums(blocks, tap_count):
    channels, row_count, col_count = blocks.shape
    flattened = blocks.reshape(channels, row_count * col_count)
    padded = jnp.concatenate([flattened, jnp.zeros((channels, row_count), blocks.dtype)], axis=1)
    diagonal = padded.reshape(channels, row_count, col_count + 1)[:, :, 1 : tap_count + 1]
    return jnp.sum(diagonal, axis=1)[:, ::-1]


def per_device(query_gate, key_gate, value_input, filter_taps, skip_gain, out_weight, cotangent):
    queries = query_gate[0]
    key_rows = key_gate[0]
    value_rows = value_input[0]
    length, channels = queries.shape
    tap_count = filter_taps.shape[1]
    seq_count = lax.axis_size("seq")
    replica_count = lax.axis_size("dp")
    norm_factor = 1.0 / math.sqrt(length * seq_count * replica_count)
    mixed = (key_rows.astype(jnp.float32) * value_rows.astype(jnp.float32)).astype(jnp.bfloat16)
    tail_rows = mixed[length - (tap_count - 1) :]
    prior = shifted(tail_rows, "seq", 1)
    extended = jnp.concatenate([jnp.zeros((1, channels), jnp.bfloat16), prior, mixed], axis=0)
    forward_windows = windows(extended, length, tap_count)
    conv = jnp.einsum(
        "cab,ibc->iac",
        forward_table(filter_taps),
        forward_windows,
        preferred_element_type=jnp.float32,
    ).reshape(length, channels)
    state = conv + skip_gain[None, :] * mixed.astype(jnp.float32)
    gated = (queries.astype(jnp.float32) * state).astype(jnp.bfloat16)
    full_cot = lax.all_gather(cotangent[0], "tp", axis=1, tiled=True)
    selected = full_cot
    grad_gated = lax.dot_general(
        selected,
        lax.all_gather(out_weight, "dp", axis=1, tiled=True),
        (((1,), (1,)), ((), ())),
        preferred_element_type=jnp.float32,
    )
    grad_query = (grad_gated * state).astype(jnp.bfloat16)
    signal = (grad_gated * queries.astype(jnp.float32)).astype(jnp.bfloat16)
    head_rows = signal[: tap_count - 1]
    later = shifted(head_rows, "seq", -1)
    signal_ext = jnp.concatenate([signal, later, jnp.zeros((1, channels), jnp.bfloat16)], axis=0)
    back = jnp.einsum(
        "cab,ibc->iac",
        backward_table(filter_taps),
        windows(signal_ext, length, tap_count),
        preferred_element_type=jnp.float32,
    ).reshape(length, channels)
    back = back + skip_gain[None, :] * signal.astype(jnp.float32)
    grad_key = (back * value_rows.astype(jnp.float32)).astype(jnp.bfloat16)
    grad_value = (back * key_rows.astype(jnp.float32)).astype(jnp.bfloat16)
    signal_blocks = signal.reshape(length // block_rows, block_rows, channels)
    blocks = jnp.einsum(
        "iac,ibc->cab", signal_blocks, forward_windows, preferred_element_type=jnp.float32
    )
    skip_term = jnp.sum(signal.astype(jnp.float32) * mixed.astype(jnp.float32), axis=0)
    filter_sum, skip_sum = lax.psum((lag_sums(blocks, tap_count), skip_term), ("seq", "dp"))
    selected = full_cot
    grad_weight = lax.psum_scatter(
        lax.dot_general(
            selected, gated, (((0,), (0,)), ((), ())), preferred_element_type=jnp.float32
        ),
        ("seq", "dp"),
        scatter_dimension=0,
        tiled=True,
    )
    return (
        grad_query[None],
        grad_key[None],
        grad_value[None],
        filter_sum * norm_factor,
        skip_sum * norm_factor,
        grad_weight * norm_factor,
    )


def solution(mesh):
    return jax.shard_map(
        per_device,
        mesh=mesh,
        in_specs=(
            P("dp", "seq", "tp"),
            P("dp", "seq", "tp"),
            P("dp", "seq", "tp"),
            P("tp", None),
            P("tp"),
            P("tp", "dp"),
            P("dp", "seq", "tp"),
        ),
        out_specs=(
            P("dp", "seq", "tp"),
            P("dp", "seq", "tp"),
            P("dp", "seq", "tp"),
            P("tp", None),
            P("tp"),
            P(("seq", "dp"), "tp"),
        ),
        check_vma=False,
    )
```

profile of v0, /device:TPU:64, one launch (start us, length us, event | category | flops | bytes accessed | tf_op | source)
XLA Modules:
  0.0 1021.4 jit_solution(6205468329109296625)
XLA Ops:
  22.1 7.0 slice.135
  29.0 12.7 %copy.93 = bf16[1024,16,144]{2,1,0:T(8,128)(2,1)} copy(bf16[1024,16,144]{0,2,1:T(8,128)(2,1)} %slice.135) | data formatting | bytes 9437184
  45.5 112.5 %all-gather.4.cloned.1.call-done = bf16[1024,4096]{1,0:T(8,128)(2,1)} async-done(((bf16[1024,2048]{1,0:T(8,128)(2,1)}), bf16[1024,4096]{1,0:T(8,128)(2,1)}) %all-gather.4.cloned.1.call-update) | async-done | bytes 8388624 | tf_op jit(solution)/shard_map/all_gather | solution.py:84
  158.0 7.5 fusion.8
  182.6 6.8 slice.120
  189.4 12.5 %copy.92 = bf16[1024,16,144]{2,1,0:T(8,128)(2,1)} copy(bf16[1024,16,144]{0,2,1:T(8,128)(2,1)} %slice.120) | data formatting | bytes 9437184
  212.9 5.8 copy.75
  218.7 5.8 copy.76
  254.6 35.9 %concatenate.45 = bf16[16,144,1024]{1,0,2:T(8,128)(2,1)} concatenate(bf16[16,16,1024]{1,0,2:T(8,128)(2,1)} %copy.74, bf16[16,16,1024]{1,0,2:T(8,128)(2,1)} %copy.75, bf16[16,16,1024]{1,0,2:T(8,128)(2,1)} %copy.76, bf16[16,16,1024]{1,0,2:T(8,128)(2,1)} %copy.77, bf16[16,16,1024]{1,0,2:T(8,128)(2,1)} %copy.78, bf16[16,16,1024]{1,0,2:T(8,128)(2,1)} %copy.79, ...), dimensions={1} | concatenate | bytes 9437184 | tf_op jit(solution)/shard_map/concatenate | solution.py:47
  290.6 11.3 %convolution_bitcast_fusion.1 = f32[16,16,1024]{1,0,2:T(8,128)} fusion(bf16[16,144,1024]{1,0,2:T(8,128)(2,1)} %concatenate.45, bf16[1024,16,144]{2,1,0:T(8,128)(2,1)} %copy.93), kind=kOutput, calls=%fused_computation.2 | convolution fusion | flops 75497472 | bytes 10485760 | tf_op jit(solution)/shard_map/cab,ibc->iac/dot_general | solution.py:93
  320.3 5.8 copy.64
  326.1 5.7 copy.65
  331.8 5.9 copy.66
  352.8 35.9 %concatenate.41 = bf16[16,144,1024]{1,0,2:T(8,128)(2,1)} concatenate(bf16[16,16,1024]{1,0,2:T(8,128)(2,1)} %copy.62, bf16[16,16,1024]{1,0,2:T(8,128)(2,1)} %copy.63, bf16[16,16,1024]{1,0,2:T(8,128)(2,1)} %copy.64, bf16[16,16,1024]{1,0,2:T(8,128)(2,1)} %copy.65, bf16[16,16,1024]{1,0,2:T(8,128)(2,1)} %copy.66, bf16[16,16,1024]{1,0,2:T(8,128)(2,1)} %copy.67, ...), dimensions={1} | concatenate | bytes 9437184 | tf_op jit(solution)/shard_map/concatenate | solution.py:47
  388.7 9.9 fusion.29
  398.6 11.3 %convolution_bitcast_fusion.2 = f32[16,16,1024]{1,0,2:T(8,128)} fusion(bf16[16,144,1024]{1,0,2:T(8,128)(2,1)} %concatenate.41, bf16[1024,16,144]{2,1,0:T(8,128)(2,1)} %copy.92), kind=kOutput, calls=%fused_computation.3 | convolution fusion | flops 75497472 | bytes 10485760 | tf_op jit(solution)/shard_map/cab,ibc->iac/dot_general | solution.py:72
  415.0 15.0 %copy.87 = f32[1024,16,144]{0,2,1:T(8,128)} copy(f32[1024,16,144]{2,1,0:T(8,128)} %fusion.29) | data formatting | bytes 18874368 | tf_op jit(solution)/shard_map/iac,ibc->cab/dot_general | solution.py:103
  430.0 9.3 concatenate.47
  439.3 10.3 %reshape.126 = f32[1024,16,145]{0,2,1:T(8,128)} reshape(f32[1024,2320]{0,1:T(8,128)} %concatenate.47) | data formatting | bytes 19005440 | tf_op jit(solution)/shard_map/reshape | solution.py:54
  463.7 8.1 convolution_bitcast_fusion
  471.8 17.5 %copy.90 = f32[4096,1024]{1,0:T(8,128)} copy(f32[4096,1024]{0,1:T(8,128)} %convolution_bitcast_fusion) | data formatting | bytes 33554432
  489.4 124.9 %psum.15 = f32[1024]{0:T(1024)S(1)} all-reduce(f32[1024]{0:T(1024)S(1)} %get-tuple-element.24), channel_id=1, replica_groups=mesh['seq'=32,'tp'=4,'dp'=2] {'seq','dp'}, use_global_device_ids=true, to_apply=%region_3.0 | all-reduce | flops 1024 | bytes 8192 | tf_op jit(solution)/shard_map/psum | solution.py:107
  614.8 22.9 %all-reduce.3.cloned.1.call-done = f32[1024,128]{0,1:T(8,128)} async-done(((f32[1024,128]{0,1:T(8,128)}), f32[1024,128]{0,1:T(8,128)}) %all-reduce.3.cloned.1.call-update) | async-done | bytes 524304 | tf_op jit(solution)/shard_map/psum | solution.py:107
  639.7 372.7 %reduce-scatter.4.cloned.1.call-done = f32[64,1024]{1,0:T(8,128)} async-done(((f32[4096,1024]{1,0:T(8,128)}), f32[64,1024]{1,0:T(8,128)}) %reduce-scatter.4.cloned.1.call-update) | async-done | bytes 262160
  (69 shorter events, 134.3 us)
Async XLA Ops:
  7.2 38.3 %all-gather.6.cloned.1.call-start = ((), (), s32[]{:S(2)}) async-start(), calls=%async_computation.3 | async-start | bytes 2621440 | tf_op jit(solution)/shard_map/all_gather | solution.py:80
  7.9 150.1 %all-gather.4.cloned.1.call-start = ((), (), s32[]{:S(2)}) async-start(), calls=%async_computation.1 | async-start | bytes 12582912 | tf_op jit(solution)/shard_map/all_gather | solution.py:84
  8.6 629.0 %all-reduce.3.cloned.1.call-start = ((), (), s32[]{:S(2)}) async-start(), calls=%async_computation.2 | async-start | bytes 1048576 | tf_op jit(solution)/shard_map/psum | solution.py:107
  29.0 129.0 %copy-start = (bf16[1,256,1024]{2,1,0:T(8,128)(2,1)S(1)}, bf16[1,256,1024]{2,1,0:T(8,128)(2,1)}, u32[]{:S(2)}) copy-start(bf16[1,256,1024]{2,1,0:T(8,128)(2,1)} %param.9) | copy-start | bytes 1572868
  29.0 129.0 %copy-start.1 = (bf16[1,256,1024]{2,1,0:T(8,128)(2,1)S(1)}, bf16[1,256,1024]{2,1,0:T(8,128)(2,1)}, u32[]{:S(2)}) copy-start(bf16[1,256,1024]{2,1,0:T(8,128)(2,1)} %param.8) | copy-start | bytes 1572868
  29.0 129.0 %copy-start.3 = (bf16[1,256,1024]{2,1,0:T(8,128)(2,1)S(1)}, bf16[1,256,1024]{2,1,0:T(8,128)(2,1)}, u32[]{:S(2)}) copy-start(bf16[1,256,1024]{2,1,0:T(8,128)(2,1)} %param.7) | copy-start | bytes 1572868
  166.2 43.8 %collective-permute-start.1 = (bf16[127,1024]{1,0:T(8,128)(2,1)}, bf16[127,1024]{1,0:T(8,128)(2,1)}, u32[]{:S(2)}, u32[]{:S(2)}) collective-permute-start(bf16[127,1024]{1,0:T(8,128)(2,1)} %slice.121), channel_id=1, source_target_pairs={{8,0},{16,8},{24,16},{32,24},{40,32},{48,40},{56,48},{64,56},{72,6... | collective-permute-start | bytes 780296 | tf_op jit(solution)/shard_map/ppermute | solution.py:13
  207.5 99.5 %collective-permute-start = (bf16[127,1024]{1,0:T(8,128)(2,1)}, bf16[127,1024]{1,0:T(8,128)(2,1)S(1)}, u32[]{:S(2)}, u32[]{:S(2)}) collective-permute-start(bf16[127,1024]{1,0:T(8,128)(2,1)} %slice.106), channel_id=1, source_target_pairs={{0,8},{8,16},{16,24},{24,32},{32,40},{40,48},{48,56},{56,64},{64,7... | collective-permute-start | bytes 780296 | tf_op jit(solution)/shard_map/ppermute | solution.py:13
  449.6 10.6 %copy-start.4 = (f32[1024]{0:T(1024)S(1)}, f32[1024]{0:T(1024)}, u32[]{:S(2)}) copy-start(f32[1024]{0:T(1024)} %param.11) | copy-start | bytes 12292
  459.9 552.6 %reduce-scatter.4.cloned.1.call-start = ((), (), s32[]{:S(2)}) async-start(), calls=%async_computation.4 | async-start | bytes 17039360
  460.2 3.5 copy-start.2
Sparse Core Ops, SparseCore 0:
  9.8 35.6 all-gather.5
  47.3 110.6 all-gather.3
  460.0 177.6 all-reduce.2
  640.1 372.3 reduce-scatter.3
where the time goes:
time: 1030 us; the launch traced here: 1020 us
  waiting for transfers between devices  513 us (50%)
  local copies, waits for them, and re-layouts  298 us (29%)
  blocking collectives  125 us (12%)
  matrix products  48 us (5%)
  other arithmetic  17.2 us (2%)
  between operations  14.2 us (1%)
    unnamed x5, waiting for transfers between devices  374 us
    psum x1, blocking collectives, per_device(): lax.psum((lag_sums(blocks, tap_count), skip_term), ('seq', 'dp'))  125 us
    all_gather x1, waiting for transfers between devices, per_device(): lax.all_gather(out_weight, 'dp', axis=1, tiled=True)  113 us
    reshape x17, local copies, waits for them, and re-layouts, windows(): extended[lower:lower + length]  90.5 us
    concatenate x2, local copies, waits for them, and re-layouts, windows(): return jnp.concatenate(pieces, axis=1)  71.9 us
    unnamed x16, local copies, waits for them, and re-layouts  45.8 us
    psum x1, waiting for transfers between devices, per_device(): lax.psum((lag_sums(blocks, tap_count), skip_term), ('seq', 'dp'))  22.9 us
  transfers between devices with their start and end apart: 6, of which 4 were waited for; matrix products, arithmetic and copies ran while one was open for 20% of the time, Pallas kernels for 0%

commit v1 on v0

--- a/solution.py
+++ b/solution.py
@@ -81,7 +81,9 @@
     selected = full_cot
     grad_gated = lax.dot_general(
         selected,
-        lax.all_gather(out_weight, "dp", axis=1, tiled=True),
+        jnp.concatenate(
+            lax.all_to_all(jnp.stack([out_weight] * lax.axis_size("dp")), "dp", 0, 0), axis=1
+        ),
         (((1,), (1,)), ((), ())),
         preferred_element_type=jnp.float32,
     )

time: 1030 us -> 999 us (0.970)
  waiting for transfers between devices: 513 us -> 461 us
    all_gather x1 -> x0, waiting for transfers between devices: 113 us -> none  [per_device(): lax.all_gather(out_weight, 'dp', axis=1, tiled=True)]
    all_to_all x0 -> x1, waiting for transfers between devices: none -> 54.8 us  [per_device(): lax.all_to_all(jnp.stack([out_weight] * lax.axis_size('dp')), 'dp', 0, 0)]
    unnamed x16 -> x19, local copies, waits for them, and re-layouts: 45.8 us -> 52.2 us
    unnamed x5 -> x4, waiting for transfers between devices: 374 us -> 374 us
where the time goes in v1:
time: 999 us; the launch traced here: 986 us
  waiting for transfers between devices  461 us (46%)
  local copies, waits for them, and re-layouts  302 us (30%)
  blocking collectives  125 us (13%)
  matrix products  47.9 us (5%)
  other arithmetic  23.7 us (2%)
  between operations  14.2 us (1%)
  starting transfers between devices  12.5 us (1%)
    unnamed x4, waiting for transfers between devices  374 us
    psum x1, blocking collectives, per_device(): lax.psum((lag_sums(blocks, tap_count), skip_term), ('seq', 'dp'))  125 us
    reshape x17, local copies, waits for them, and re-layouts, windows(): extended[lower:lower + length]  90.5 us
    concatenate x2, local copies, waits for them, and re-layouts, windows(): return jnp.concatenate(pieces, axis=1)  71.9 us
    all_to_all x1, waiting for transfers between devices, per_device(): lax.all_to_all(jnp.stack([out_weight] * lax.axis_size('dp')), 'dp', 0, 0)  54.8 us
    unnamed x19, local copies, waits for them, and re-layouts  52.2 us
    psum x1, waiting for transfers between devices, per_device(): lax.psum((lag_sums(blocks, tap_count), skip_term), ('seq', 'dp'))  22.9 us
  transfers between devices with their start and end apart: 6, of which 4 were waited for; matrix products, arithmetic and copies ran while one was open for 20% of the time, Pallas kernels for 0%

profile of v1, /device:TPU:64, one launch (start us, length us, event | category | flops | bytes accessed | tf_op | source)
XLA Modules:
  0.0 986.3 jit_solution(14131066953476761637)
XLA Ops:
  7.2 6.4 copy.63
  13.6 7.5 pad_maximum_fusion
  21.0 7.1 all-to-all-start
  38.6 6.8 slice.135
  45.4 12.8 %copy.95 = bf16[1024,16,144]{2,1,0:T(8,128)(2,1)} copy(bf16[1024,16,144]{0,2,1:T(8,128)(2,1)} %slice.135) | data formatting | bytes 9437184
  58.2 9.2 all-gather.3.cloned.1.call-done
  67.4 54.8 %all-to-all-done = bf16[2,1024,2048]{1,2,0:T(8,128)(2,1)} async-done(((bf16[2,1024,2048]{1,2,0:T(8,128)(2,1)}), bf16[2,1024,2048]{1,2,0:T(8,128)(2,1)}, u32[]{:S(2)}, u32[]{:S(2)}) %all-to-all-start) | async-done | bytes 8388640 | tf_op jit(solution)/shard_map/all_to_all | solution.py:85
  122.2 7.4 fusion.11
  146.7 6.8 slice.120
  153.5 12.5 %copy.94 = bf16[1024,16,144]{2,1,0:T(8,128)(2,1)} copy(bf16[1024,16,144]{0,2,1:T(8,128)(2,1)} %slice.120) | data formatting | bytes 9437184
  218.8 35.9 %concatenate.45 = bf16[16,144,1024]{1,0,2:T(8,128)(2,1)} concatenate(bf16[16,16,1024]{1,0,2:T(8,128)(2,1)} %copy.76, bf16[16,16,1024]{1,0,2:T(8,128)(2,1)} %copy.77, bf16[16,16,1024]{1,0,2:T(8,128)(2,1)} %copy.78, bf16[16,16,1024]{1,0,2:T(8,128)(2,1)} %copy.79, bf16[16,16,1024]{1,0,2:T(8,128)(2,1)} %copy.80, bf16[16,16,1024]{1,0,2:T(8,128)(2,1)} %copy.81, ...), dimensions={1} | concatenate | bytes 9437184 | tf_op jit(solution)/shard_map/concatenate | solution.py:47
  254.7 11.3 %convolution_bitcast_fusion.1 = f32[16,16,1024]{1,0,2:T(8,128)} fusion(bf16[16,144,1024]{1,0,2:T(8,128)(2,1)} %concatenate.45, bf16[1024,16,144]{2,1,0:T(8,128)(2,1)} %copy.95), kind=kOutput, calls=%fused_computation.3 | convolution fusion | flops 75497472 | bytes 10485760 | tf_op jit(solution)/shard_map/cab,ibc->iac/dot_general | solution.py:95
  295.9 5.9 copy.68
  316.9 35.9 %concatenate.41 = bf16[16,144,1024]{1,0,2:T(8,128)(2,1)} concatenate(bf16[16,16,1024]{1,0,2:T(8,128)(2,1)} %copy.64, bf16[16,16,1024]{1,0,2:T(8,128)(2,1)} %copy.65, bf16[16,16,1024]{1,0,2:T(8,128)(2,1)} %copy.66, bf16[16,16,1024]{1,0,2:T(8,128)(2,1)} %copy.67, bf16[16,16,1024]{1,0,2:T(8,128)(2,1)} %copy.68, bf16[16,16,1024]{1,0,2:T(8,128)(2,1)} %copy.69, ...), dimensions={1} | concatenate | bytes 9437184 | tf_op jit(solution)/shard_map/concatenate | solution.py:47
  352.9 9.9 %fusion.32 = f32[1024,16,144]{2,1,0:T(8,128)} fusion(bf16[16,16,1024]{1,0,2:T(8,128)(2,1)} %copy.76, bf16[16,144,1024]{1,0,2:T(8,128)(2,1)} %concatenate.41), kind=kOutput, calls=%fused_computation.77 | convolution fusion | flops 75497472 | bytes 14680064 | tf_op jit(solution)/shard_map/iac,ibc->cab/dot_general | solution.py:105
  362.7 11.3 %convolution_bitcast_fusion.2 = f32[16,16,1024]{1,0,2:T(8,128)} fusion(bf16[16,144,1024]{1,0,2:T(8,128)(2,1)} %concatenate.41, bf16[1024,16,144]{2,1,0:T(8,128)(2,1)} %copy.94), kind=kOutput, calls=%fused_computation.4 | convolution fusion | flops 75497472 | bytes 10485760 | tf_op jit(solution)/shard_map/cab,ibc->iac/dot_general | solution.py:72
  379.1 15.0 %copy.89 = f32[1024,16,144]{0,2,1:T(8,128)} copy(f32[1024,16,144]{2,1,0:T(8,128)} %fusion.32) | data formatting | bytes 18874368 | tf_op jit(solution)/shard_map/iac,ibc->cab/dot_general | solution.py:105
  394.2 9.3 concatenate.47
  403.4 10.3 %reshape.134 = f32[1024,16,145]{0,2,1:T(8,128)} reshape(f32[1024,2320]{0,1:T(8,128)} %concatenate.47) | data formatting | bytes 19005440 | tf_op jit(solution)/shard_map/reshape | solution.py:54
  427.9 8.1 convolution_bitcast_fusion
  436.0 17.5 %copy.92 = f32[4096,1024]{1,0:T(8,128)} copy(f32[4096,1024]{0,1:T(8,128)} %convolution_bitcast_fusion) | data formatting | bytes 33554432
  453.5 125.4 %psum.15 = f32[1024]{0:T(1024)S(1)} all-reduce(f32[1024]{0:T(1024)S(1)} %get-tuple-element.24), channel_id=1, replica_groups=mesh['seq'=32,'tp'=4,'dp'=2] {'seq','dp'}, use_global_device_ids=true, to_apply=%region_3.0 | all-reduce | flops 1024 | bytes 8192 | tf_op jit(solution)/shard_map/psum | solution.py:109
  579.5 22.9 %all-reduce.3.cloned.1.call-done = f32[1024,128]{0,1:T(8,128)} async-done(((f32[1024,128]{0,1:T(8,128)}), f32[1024,128]{0,1:T(8,128)}) %all-reduce.3.cloned.1.call-update) | async-done | bytes 524304 | tf_op jit(solution)/shard_map/psum | solution.py:109
  604.4 373.0 %reduce-scatter.4.cloned.1.call-done = f32[64,1024]{1,0:T(8,128)} async-done(((f32[4096,1024]{1,0:T(8,128)}), f32[64,1024]{1,0:T(8,128)}) %reduce-scatter.4.cloned.1.call-update) | async-done | bytes 262160
  (72 shorter events, 149.2 us)
Async XLA Ops:
  21.0 8.0 copy-start.3
  21.0 101.2 %all-to-all-start = ((bf16[2,1024,2048]{1,2,0:T(8,128)(2,1)}), bf16[2,1024,2048]{1,2,0:T(8,128)(2,1)}, u32[]{:S(2)}, u32[]{:S(2)}) async-start(bf16[2,1024,2048]{1,2,0:T(8,128)(2,1)} %pad_maximum_fusion), calls=%async_computation | async-start | bytes 16777216 | tf_op jit(solution)/shard_map/all_to_all | solution.py:85
  28.1 39.3 %all-gather.3.cloned.1.call-start = ((), (), s32[]{:S(2)}) async-start(), calls=%async_computation.3 | async-start | bytes 2621440 | tf_op jit(solution)/shard_map/all_gather | solution.py:80
  28.9 573.5 %all-reduce.3.cloned.1.call-start = ((), (), s32[]{:S(2)}) async-start(), calls=%async_computation.2 | async-start | bytes 1048576 | tf_op jit(solution)/shard_map/psum | solution.py:109
  45.4 76.8 %copy-start = (bf16[1,256,1024]{2,1,0:T(8,128)(2,1)S(1)}, bf16[1,256,1024]{2,1,0:T(8,128)(2,1)}, u32[]{:S(2)}) copy-start(bf16[1,256,1024]{2,1,0:T(8,128)(2,1)} %param.9) | copy-start | bytes 1572868
  45.4 76.8 %copy-start.1 = (bf16[1,256,1024]{2,1,0:T(8,128)(2,1)S(1)}, bf16[1,256,1024]{2,1,0:T(8,128)(2,1)}, u32[]{:S(2)}) copy-start(bf16[1,256,1024]{2,1,0:T(8,128)(2,1)} %param.8) | copy-start | bytes 1572868
  45.4 76.8 %copy-start.4 = (bf16[1,256,1024]{2,1,0:T(8,128)(2,1)S(1)}, bf16[1,256,1024]{2,1,0:T(8,128)(2,1)}, u32[]{:S(2)}) copy-start(bf16[1,256,1024]{2,1,0:T(8,128)(2,1)} %param.7) | copy-start | bytes 1572868
  130.4 43.8 %collective-permute-start.1 = (bf16[127,1024]{1,0:T(8,128)(2,1)}, bf16[127,1024]{1,0:T(8,128)(2,1)}, u32[]{:S(2)}, u32[]{:S(2)}) collective-permute-start(bf16[127,1024]{1,0:T(8,128)(2,1)} %slice.121), channel_id=1, source_target_pairs={{8,0},{16,8},{24,16},{32,24},{40,32},{48,40},{56,48},{64,56},{72,6... | collective-permute-start | bytes 780296 | tf_op jit(solution)/shard_map/ppermute | solution.py:13
  171.6 99.5 %collective-permute-start = (bf16[127,1024]{1,0:T(8,128)(2,1)}, bf16[127,1024]{1,0:T(8,128)(2,1)S(1)}, u32[]{:S(2)}, u32[]{:S(2)}) collective-permute-start(bf16[127,1024]{1,0:T(8,128)(2,1)} %slice.106), channel_id=1, source_target_pairs={{0,8},{8,16},{16,24},{24,32},{32,40},{40,48},{48,56},{56,64},{64,7... | collective-permute-start | bytes 780296 | tf_op jit(solution)/shard_map/ppermute | solution.py:13
  413.8 10.6 %copy-start.5 = (f32[1024]{0:T(1024)S(1)}, f32[1024]{0:T(1024)}, u32[]{:S(2)}) copy-start(f32[1024]{0:T(1024)} %param.11) | copy-start | bytes 12292
  424.0 553.4 %reduce-scatter.4.cloned.1.call-start = ((), (), s32[]{:S(2)}) async-start(), calls=%async_computation.4 | async-start | bytes 17039360
  424.3 3.5 copy-start.2
Sparse Core Ops, SparseCore 0:
  30.8 36.6 all-gather.2
  424.1 178.1 all-reduce.2
  604.9 372.4 reduce-scatter.3
